TPU v7x, 32 devices: a whole 2x2x4 slice. The times are simulated.
32 devices in a mesh: cell: 2 (over x), seq: 16 (over z, y, core).
Axes of the slice: x: 2, y: 2, z: 4, core: 2. Of those that a mesh axis runs over, the one named last changes fastest.
Arguments:
- queries: bfloat16 [128, 6144], P(('cell', 'seq')), parts along dimension 0, may hold values from -500 to 500
- keys: bfloat16 [256, 128, 1024], P(('cell', 'seq')), parts along dimension 0, may hold values from -6 to 6
- values: bfloat16 [256, 128, 1024], P(('cell', 'seq')), parts along dimension 0, may hold values from -6 to 6
- page_request: int32 [256], P(('cell', 'seq')), parts along dimension 0, may hold values from 0 to 63, as said below
- page_fill: int32 [256], P(('cell', 'seq')), parts along dimension 0, may hold values from 0 to 128
Outputs:
- attended: bfloat16 [128, 6144], P(('cell', 'seq')), parts along dimension 0
There are 2 independent parts, one for each index of `cell`. A program takes and returns all parts, laid end to end along the dimension named above; each array names one. Nothing has to cross between parts.
Inputs may be any that keep to these rules, and one draw needn't show every extreme that they name: `page_request`: every request has at least one page with a live slot. Request r's home is index r // 4 of seq; among one device's pages, the requests of any one home are at most 2 distinct ones, and some device reaches that.
All inputs are finite; a program needn't handle non-finite values.
Results may differ from a plain program's by a relative error of at most 0.0035.
Values may be sent and summed in bfloat16 or wider, within the bound.
A program may use at most 64 MiB of HBM per device.

v0:
```python
import jax
import jax.numpy as jnp
from jax import lax
from jax.sharding import PartitionSpec as P

HEADS = 48
KV_HEADS = 8
HEAD_DIM = 128
GROUP = 6


FLOOR = -30000.0


def page_partials(everyone, keys, values, page_request, page_fill):
    pages, page_len = (keys.shape[0], keys.shape[1])
    chosen = jnp.take(everyone, page_request, axis=0).reshape(pages, KV_HEADS, GROUP, HEAD_DIM)
    keyed = keys.reshape(pages, page_len, KV_HEADS, HEAD_DIM)
    valued = values.reshape(pages, page_len, KV_HEADS, HEAD_DIM)
    scores = jnp.einsum(
        "pkgd,ptkd->pkgt", chosen, keyed, preferred_element_type=jnp.float32
    ) * HEAD_DIM ** (-0.5)
    live = (lax.broadcasted_iota(jnp.int32, (pages, page_len), 1) < page_fill[:, None])[
        :, None, None, :
    ]
    page_max = jnp.max(jnp.where(live, scores, FLOOR), axis=3)
    weights = jnp.where(live, jnp.exp(scores - page_max[..., None]), 0.0).astype(jnp.bfloat16)
    page_sum = jnp.sum(weights.astype(jnp.float32), axis=3).reshape(pages, HEADS)
    page_acc = jnp.einsum(
        "pkgt,ptkd->pkgd", weights, valued, preferred_element_type=jnp.float32
    ).reshape(pages, HEADS, HEAD_DIM)
    page_max = page_max.reshape(pages, HEADS)
    same = page_request[:, None] == page_request[None, :]
    slot_max = jnp.max(jnp.where(same[:, :, None], page_max[None], FLOOR), axis=1)
    factor = jnp.where(same[:, :, None], jnp.exp(page_max[None] - slot_max[:, None, :]), 0.0)
    slot_sum = jnp.sum(factor * page_sum[None], axis=1)
    slot_acc = jnp.einsum("qph,phd->qhd", factor, page_acc, precision=lax.Precision.HIGHEST)
    partial_value = (slot_acc / jnp.maximum(slot_sum, 1.0)[..., None]).astype(jnp.bfloat16)
    earlier = lax.broadcasted_iota(jnp.int32, (pages, pages), 1) < lax.broadcasted_iota(
        jnp.int32, (pages, pages), 0
    )
    leader = jnp.logical_not(jnp.any(same & earlier, axis=1))
    return (partial_value.reshape(pages, -1), slot_max, slot_sum, leader, earlier)


def select_rows(place, partial_value, slot_max, slot_sum):
    rows_partial = jnp.dot(
        place.astype(jnp.bfloat16), partial_value, preferred_element_type=jnp.float32
    ).astype(jnp.bfloat16)
    rows_max = jnp.max(jnp.where(place[:, :, None], slot_max[None], FLOOR), axis=1)
    rows_sum = jnp.sum(jnp.where(place[:, :, None], slot_sum[None], 0.0), axis=1)
    return (rows_partial, rows_max, rows_sum)


def body(queries, keys, values, page_request, page_fill):
    req_dev = queries.shape[0]
    everyone = lax.all_gather(queries, "seq", axis=0, tiled=True)
    requests, width = everyone.shape
    pages = keys.shape[0]
    partial_value, slot_max, slot_sum, leader, earlier = page_partials(
        everyone, keys, values, page_request, page_fill
    )
    homes = lax.axis_size("seq")
    capacity = min(2, req_dev)
    home_of = page_request // req_dev
    same_home = home_of[:, None] == home_of[None, :]
    rank = jnp.sum((same_home & earlier & leader[None, :]).astype(jnp.int32), axis=1)
    target = home_of * capacity + rank
    send = (
        target[None, :] == lax.broadcasted_iota(jnp.int32, (homes * capacity, pages), 0)
    ) & leader[None, :]
    out_partial, out_max, out_sum = select_rows(send, partial_value, slot_max, slot_sum)
    local_id = (page_request % req_dev).astype(jnp.float32) + 1.0
    out_id = jnp.sum(jnp.where(send, local_id[None, :], 0.0), axis=1) - 1.0
    got_partial, got_max, got_sum, got_id = (
        lax.all_to_all(
            out_partial.reshape(homes, capacity, width).astype(jnp.float32),
            "seq",
            split_axis=0,
            concat_axis=0,
            tiled=True,
        ).astype(jnp.bfloat16),
        lax.all_to_all(
            out_max.reshape(homes, capacity, HEADS), "seq", split_axis=0, concat_axis=0, tiled=True
        ),
        lax.all_to_all(
            out_sum.reshape(homes, capacity, HEADS), "seq", split_axis=0, concat_axis=0, tiled=True
        ),
        lax.all_to_all(
            out_id.reshape(homes, capacity), "seq", split_axis=0, concat_axis=0, tiled=True
        ),
    )
    count = homes * capacity
    got_partial = got_partial.reshape(count, HEADS, HEAD_DIM)
    got_max = got_max.reshape(count, HEADS)
    got_sum = got_sum.reshape(count, HEADS)
    got_id = got_id.reshape(count)
    mine = got_id[None, :] == lax.broadcasted_iota(jnp.int32, (req_dev, count), 0).astype(
        jnp.float32
    )
    top = jnp.max(jnp.where(mine[:, :, None], got_max[None], FLOOR), axis=1)
    slot_top = jnp.sum(jnp.where(mine[:, :, None], top[:, None, :], 0.0), axis=0)
    share = got_sum * jnp.exp(got_max - slot_top)
    weighted = share[..., None] * got_partial.astype(jnp.float32)
    picker = mine.astype(jnp.float32)
    numer = jnp.einsum("rs,shd->rhd", picker, weighted, precision=lax.Precision.HIGHEST)
    denom = jnp.einsum("rs,sh->rh", picker, share, precision=lax.Precision.HIGHEST)
    return (numer / denom[..., None]).reshape(-1, width).astype(jnp.bfloat16)


def solution(mesh):
    placed = (
        P(("cell", "seq"), None),
        P(("cell", "seq"), None, None),
        P(("cell", "seq"), None, None),
        P(("cell", "seq")),
        P(("cell", "seq")),
    )
    return jax.shard_map(
        body, mesh=mesh, in_specs=placed, out_specs=P(("cell", "seq"), None), check_vma=False
    )
```

profile of v0, /device:TPU:0, one launch (start us, length us, event | category | flops | bytes accessed | tf_op | source)
XLA Modules:
  0.0 83.5 jit_solution(16627418202317567444)
XLA Ops:
  0.0 0.8 and_select_fusion.1
  0.8 0.9 %fusion.31 = (pred[8]{0:T(512)(128)(4,1)S(1)}, pred[8,8]{1,0:T(8,128)(4,1)S(1)}) fusion(s32[8]{0:T(128)} %param.8), kind=kLoop, calls=%fused_computation.53 | loop fusion | flops 248 | bytes 104 | tf_op jit(solution)/shard_map/reduce_or | solution.py:42
  1.7 0.7 fusion.35
  2.7 0.7 sub.42
  3.4 7.4 %all-to-all-start = ((f32[16,1,2]{2,1,0:T(1,128)}), f32[16,1,2]{2,1,0:T(1,128)S(1)}, u32[]{:S(2)}, u32[]{:S(2)}) async-start(f32[16,1,2]{2,1,0:T(1,128)} %bitcast), calls=%async_computation | async-start | bytes 16384 | tf_op jit(solution)/shard_map/all_to_all | solution.py:89
  10.8 0.7 compare_and_fusion
  11.5 0.7 iota_compare_fusion
  12.3 25.5 %all-gather = bf16[16,4,6144]{2,1,0:T(4,128)(2,1)} all-gather(bf16[1,4,6144]{2,1,0:T(4,128)(2,1)} %bitcast.50), channel_id=1, replica_groups=mesh['cell'=2,'seq'=16] {'seq'}, dimensions={0}, use_global_device_ids=true | all-gather | bytes 835584 | tf_op jit(solution)/shard_map/all_gather | solution.py:57
  37.8 1.6 %reshape.207 = bf16[64,6144]{1,0:T(8,128)(2,1)S(1)} reshape(bf16[16,4,6144]{2,1,0:T(4,128)(2,1)} %all-gather) | data formatting | bytes 1572864
  39.4 0.6 gather_fusion
  40.0 1.3 %select_reduce_fusion = (f32[8,8,6]{2,1,0:T(8,128)S(1)}, f32[8,8,6,128]{3,2,1,0:T(8,128)S(1)}) fusion(pred[8,128]{1,0:T(8,128)(4,1)S(1)} %iota_compare_fusion, bf16[8,8,6,128]{3,0,2,1:T(8,128)(2,1)S(1)} %bitcast.46, pred[8]{0:T(512)(128)(4,1)S(1)} %compare_and_fusion, bf16[8,128,1024]{2,1,0:T(8,128)(2,1)S(1)} %copy-done), kind=kOutput, calls=%fused_computation.24 | convolution fusion | flops 12779136 | bytes 2394632 | tf_op jit(solution)/shard_map/pkgd,ptkd->pkgt/dot_general | solution.py:20
  42.4 2.3 %fusion.2 = f32[8,8,6,128]{3,2,1,0:T(8,128)S(1)} fusion(f32[8,8,6,128]{3,2,1,0:T(8,128)S(1)} %get-tuple-element.12, f32[8,8,6]{2,1,0:T(8,128)S(1)} %get-tuple-element.11, pred[8,128]{1,0:T(8,128)(4,1)S(1)} %iota_compare_fusion, bf16[8,128,1024]{2,1,0:T(8,128)(2,1)} %param.7), kind=kOutput, calls=%fused_computation.4 | convolution fusion | flops 12730368 | bytes 2492928 | tf_op jit(solution)/shard_map/pkgt,ptkd->pkgd/dot_general | solution.py:29
  44.9 0.5 fusion.13
  45.5 0.8 select_reduce_fusion.2
  46.2 3.5 %all-to-all-start.1 = ((f32[16,2,48]{2,1,0:T(2,128)}), f32[16,2,48]{2,1,0:T(2,128)S(1)}, u32[]{:S(2)}, u32[]{:S(2)}) async-start(f32[16,2,48]{2,1,0:T(2,128)} %bitcast.4), calls=%async_computation.1 | async-start | bytes 32768 | tf_op jit(solution)/shard_map/all_to_all | solution.py:86
  50.1 6.1 %all-to-all-done.1 = f32[16,2,48]{2,1,0:T(2,128)S(1)} async-done(((f32[16,2,48]{2,1,0:T(2,128)}), f32[16,2,48]{2,1,0:T(2,128)S(1)}, u32[]{:S(2)}, u32[]{:S(2)}) %all-to-all-start.1) | async-done | bytes 6176 | tf_op jit(solution)/shard_map/all_to_all | solution.py:86
  56.2 3.5 %all-to-all-start.2 = ((f32[16,2,48]{2,1,0:T(2,128)}), f32[16,2,48]{2,1,0:T(2,128)S(1)}, u32[]{:S(2)}, u32[]{:S(2)}) async-start(f32[16,2,48]{2,1,0:T(2,128)} %bitcast.6), calls=%async_computation.2 | async-start | bytes 32768 | tf_op jit(solution)/shard_map/all_to_all | solution.py:83
  59.7 1.0 %reshape.195 = bf16[16,2,6144]{2,1,0:T(2,128)(2,1)} reshape(bf16[32,6144]{1,0:T(8,128)(2,1)S(1)} %fusion.1) | data formatting | bytes 786432 | tf_op jit(solution)/shard_map/convert_element_type | solution.py:77
  60.7 0.6 broadcast.151
  61.3 0.6 reduce.3
  62.0 4.1 %all-to-all-done.2 = f32[16,2,48]{2,1,0:T(2,128)S(1)} async-done(((f32[16,2,48]{2,1,0:T(2,128)}), f32[16,2,48]{2,1,0:T(2,128)S(1)}, u32[]{:S(2)}, u32[]{:S(2)}) %all-to-all-start.2) | async-done | bytes 6176 | tf_op jit(solution)/shard_map/all_to_all | solution.py:83
  66.2 3.6 %all-to-all-start.3 = ((bf16[16,2,6144]{2,1,0:T(2,128)(2,1)}), bf16[16,2,6144]{2,1,0:T(2,128)(2,1)S(1)}, u32[]{:S(2)}, u32[]{:S(2)}) async-start(bf16[16,2,6144]{2,1,0:T(2,128)(2,1)} %reshape.195), calls=%async_computation.3 | async-start | bytes 786432 | tf_op jit(solution)/shard_map/all_to_all | solution.py:76
  70.2 11.7 %all-to-all-done.3 = bf16[16,2,6144]{2,1,0:T(2,128)(2,1)S(1)} async-done(((bf16[16,2,6144]{2,1,0:T(2,128)(2,1)}), bf16[16,2,6144]{2,1,0:T(2,128)(2,1)S(1)}, u32[]{:S(2)}, u32[]{:S(2)}) %all-to-all-start.3) | async-done | bytes 393248 | tf_op jit(solution)/shard_map/all_to_all | solution.py:76
  82.4 1.2 %fusion.15 = bf16[4,6144]{1,0:T(4,128)(2,1)} fusion(f32[32,48,128]{2,1,0:T(8,128)S(1)} %broadcast_multiply_fusion, f32[4,48]{0,1:T(8,128)S(1)} %fusion.42, pred[4,32]{1,0:T(4,128)(4,1)S(1)} %broadcast_compare_fusion.1), kind=kOutput, calls=%fused_computation.17 | convolution fusion | flops 9486336 | bytes 836480 | tf_op jit(solution)/shard_map/rs,shd->rhd/dot_general | solution.py:106
  (31 shorter events, 3.0 us)
Async XLA Ops:
  0.0 40.0 %copy-start = (bf16[8,128,1024]{2,1,0:T(8,128)(2,1)S(1)}, bf16[8,128,1024]{2,1,0:T(8,128)(2,1)}, u32[]{:S(2)}) copy-start(bf16[8,128,1024]{2,1,0:T(8,128)(2,1)} %param.6) | copy-start | bytes 6291460
  3.4 42.9 %all-to-all-start = ((f32[16,1,2]{2,1,0:T(1,128)}), f32[16,1,2]{2,1,0:T(1,128)S(1)}, u32[]{:S(2)}, u32[]{:S(2)}) async-start(f32[16,1,2]{2,1,0:T(1,128)} %bitcast), calls=%async_computation | async-start | bytes 16384 | tf_op jit(solution)/shard_map/all_to_all | solution.py:89
  46.2 10.0 %all-to-all-start.1 = ((f32[16,2,48]{2,1,0:T(2,128)}), f32[16,2,48]{2,1,0:T(2,128)S(1)}, u32[]{:S(2)}, u32[]{:S(2)}) async-start(f32[16,2,48]{2,1,0:T(2,128)} %bitcast.4), calls=%async_computation.1 | async-start | bytes 32768 | tf_op jit(solution)/shard_map/all_to_all | solution.py:86
  56.2 10.0 %all-to-all-start.2 = ((f32[16,2,48]{2,1,0:T(2,128)}), f32[16,2,48]{2,1,0:T(2,128)S(1)}, u32[]{:S(2)}, u32[]{:S(2)}) async-start(f32[16,2,48]{2,1,0:T(2,128)} %bitcast.6), calls=%async_computation.2 | async-start | bytes 32768 | tf_op jit(solution)/shard_map/all_to_all | solution.py:83
  66.2 15.7 %all-to-all-start.3 = ((bf16[16,2,6144]{2,1,0:T(2,128)(2,1)}), bf16[16,2,6144]{2,1,0:T(2,128)(2,1)S(1)}, u32[]{:S(2)}, u32[]{:S(2)}) async-start(bf16[16,2,6144]{2,1,0:T(2,128)(2,1)} %reshape.195), calls=%async_computation.3 | async-start | bytes 786432 | tf_op jit(solution)/shard_map/all_to_all | solution.py:76
where the time goes:
time: 84 us; the launch traced here: 83.5 us
  blocking collectives  25.5 us (30%)
  waiting for transfers between devices  21.9 us (26%)
  starting transfers between devices  18 us (21%)
  other arithmetic  6.64 us (8%)
  matrix products  5.87 us (7%)
  local copies, waits for them, and re-layouts  5.42 us (6%)
    all_gather x1, blocking collectives, body(): everyone = lax.all_gather(queries, 'seq', axis=0, tiled=True)  25.5 us
    all_to_all x1, waiting for transfers between devices, body(): lax.all_to_all(out_partial.reshape(homes, capacity, width).astype(jnp.flo...  11.7 us
    all_to_all x1, starting transfers between devices, body(): lax.all_to_all(out_id.reshape(homes, capacity), 'seq', split_axis=0, conc...  7.41 us
    all_to_all x1, waiting for transfers between devices, body(): lax.all_to_all(out_sum.reshape(homes, capacity, HEADS), 'seq', split_axis...  6.09 us
    all_to_all x1, waiting for transfers between devices, body(): lax.all_to_all(out_max.reshape(homes, capacity, HEADS), 'seq', split_axis...  4.14 us
    all_to_all x1, starting transfers between devices, body(): lax.all_to_all(out_partial.reshape(homes, capacity, width).astype(jnp.flo...  3.55 us
    all_to_all x1, starting transfers between devices, body(): lax.all_to_all(out_max.reshape(homes, capacity, HEADS), 'seq', split_axis...  3.5 us
    all_to_all x1, starting transfers between devices, body(): lax.all_to_all(out_sum.reshape(homes, capacity, HEADS), 'seq', split_axis...  3.49 us
  transfers between devices with their start and end apart: 4, of which 3 were waited for; matrix products, arithmetic and copies ran while one was open for 15% of the time, Pallas kernels for 0%

commit v1 on v0

v1 whole, which is shorter than its diff:
```python
import functools

import jax
import jax.numpy as jnp
from jax import lax
from jax.experimental import pallas as pl
from jax.experimental.pallas import tpu as pltpu
from jax.sharding import PartitionSpec as P

HEAD_DIM = 128
KV_HEADS = 8
FLOOR = -30000.0
SLOTS = 2


def kernel(
    n, req_ref, fill_ref, q_ref, k_hbm, v_hbm, o_ref,
    kbuf, vbuf, qbuf, acc, pbuf, stat, sdata, sstat, rdata, rstat, leaders,
    k_sem, v_sem, q_recv, q_far, q_pair, q_sib, d_send, d_recv, s_send, s_recv,
):
    pages = k_hbm.shape[0]
    req_dev, width = q_ref.shape
    heads = width // HEAD_DIM
    group = heads // KV_HEADS
    far_n = n // 4
    me = lax.axis_index("seq")

    def remote(src, dst, send, recv, peer):
        return pltpu.make_async_remote_copy(
            src_ref=src, dst_ref=dst, send_sem=send, recv_sem=recv,
            device_id={"seq": peer}, device_id_type=pl.DeviceIdType.MESH,
        )

    barrier = pltpu.get_barrier_semaphore()

    def greet(d, _):
        pl.semaphore_signal(
            barrier, inc=1, device_id={"seq": lax.rem(me + d, n)},
            device_id_type=pl.DeviceIdType.MESH,
        )
        return 0

    lax.fori_loop(1, n, greet, 0)
    for p in range(pages):
        pltpu.make_async_copy(k_hbm.at[p], kbuf.at[p], k_sem.at[p]).start()
    for p in range(pages):
        pltpu.make_async_copy(v_hbm.at[p], vbuf.at[p], v_sem.at[p]).start()

    mine = q_ref[...].astype(jnp.float32)
    qbuf[me] = mine.reshape(req_dev, heads, HEAD_DIM).astype(jnp.bfloat16)
    pl.semaphore_wait(barrier, n - 1)

    far = me // 4
    place = lax.rem(me, 4)
    other = lax.rem(place + 2, 4)
    pair = far * 4 + other
    sibling = me + 1 - 2 * lax.rem(me, 2)

    def far_copy(k, owner, peer):
        return remote(qbuf.at[owner], qbuf.at[owner], q_far.at[k], q_recv.at[owner], peer)

    def pair_copy(k, owner):
        return remote(qbuf.at[owner], qbuf.at[owner], q_pair.at[k], q_recv.at[owner], pair)

    def sib_copy(k, owner):
        return remote(qbuf.at[owner], qbuf.at[owner], q_sib.at[k], q_recv.at[owner], sibling)

    def start_far(k, _):
        far_copy(k, me, lax.rem(far + k, far_n) * 4 + place).start()
        return 0

    lax.fori_loop(1, far_n, start_far, 0)
    pair_copy(0, me).start()
    sib_copy(0, me).start()

    def lead(g, _):
        first = jnp.int32(pages)
        held = jnp.int32(-1)
        for p in reversed(range(pages)):
            hit = req_ref[p] // req_dev == g
            first = jnp.where(hit, p, first)
            held = jnp.where(hit, req_ref[p], held)
        second = jnp.int32(pages)
        for p in reversed(range(pages)):
            hit = jnp.logical_and(req_ref[p] // req_dev == g, req_ref[p] != held)
            second = jnp.where(hit, p, second)
        leaders[SLOTS * g] = first
        leaders[SLOTS * g + 1] = second
        return 0

    lax.fori_loop(0, n, lead, 0)

    def pass_far(k, _):
        owner = lax.rem(far + far_n - k, far_n) * 4 + place
        far_copy(k, owner, owner).wait_recv()
        pair_copy(k, owner).start()
        sib_copy(k, owner).start()
        return 0

    lax.fori_loop(1, far_n, pass_far, 0)

    def pass_pair(k, _):
        owner = lax.rem(far + far_n - k, far_n) * 4 + other
        pair_copy(k, owner).wait_recv()
        sib_copy(far_n + k, owner).start()
        return 0

    lax.fori_loop(0, far_n, pass_pair, 0)

    def wait_sib(k, _):
        owner = 2 * k + lax.rem(sibling, 2)
        sib_copy(k, owner).wait_recv()
        return 0

    lax.fori_loop(0, n // 2, wait_sib, 0)

    lane = lax.broadcasted_iota(jnp.int32, (heads, HEAD_DIM), 1)
    key_head = lax.broadcasted_iota(jnp.int32, (heads, HEAD_DIM), 0) // group
    flat = (heads, HEAD_DIM)
    maxes, sums = [], []
    for p in range(pages):
        r = req_ref[p]
        q = qbuf[r // req_dev, lax.rem(r, req_dev)]
        wide = jnp.concatenate(
            [jnp.where(key_head == k, q, jnp.zeros_like(q)) for k in range(KV_HEADS)], axis=1
        )
        pltpu.make_async_copy(k_hbm.at[p], kbuf.at[p], k_sem.at[p]).wait()
        score = lax.dot_general(
            wide, kbuf[p], (((1,), (1,)), ((), ())), preferred_element_type=jnp.float32
        ) * HEAD_DIM ** (-0.5)
        live = lax.broadcasted_iota(jnp.int32, score.shape, 1) < fill_ref[p]
        top = jnp.max(jnp.where(live, score, FLOOR), axis=1, keepdims=True)
        weight = jnp.where(live, jnp.exp(score - top), 0.0).astype(jnp.bfloat16)
        total = jnp.sum(weight.astype(jnp.float32), axis=1, keepdims=True)
        pltpu.make_async_copy(v_hbm.at[p], vbuf.at[p], v_sem.at[p]).wait()
        mixed = jnp.dot(weight, vbuf[p], preferred_element_type=jnp.float32)
        out = jnp.zeros(flat, jnp.float32)
        for k in range(KV_HEADS):
            out = jnp.where(key_head == k, mixed[:, k * HEAD_DIM:(k + 1) * HEAD_DIM], out)
        acc[p] = out
        maxes.append(jnp.broadcast_to(top, flat))
        sums.append(jnp.broadcast_to(total, flat))

    packed = jnp.zeros(flat, jnp.float32)
    for p in range(pages):
        same = [req_ref[p] == req_ref[q] for q in range(pages)]
        slot_max = jnp.full(flat, FLOOR, jnp.float32)
        for q in range(pages):
            slot_max = jnp.maximum(slot_max, jnp.where(same[q], maxes[q], FLOOR))
        slot_sum = jnp.zeros(flat, jnp.float32)
        slot_acc = jnp.zeros(flat, jnp.float32)
        for q in range(pages):
            factor = jnp.where(same[q], jnp.exp(maxes[q] - slot_max), 0.0)
            slot_sum += factor * sums[q]
            slot_acc += factor * acc[q]
        pbuf[p] = (slot_acc / jnp.maximum(slot_sum, 1.0)).astype(jnp.bfloat16)
        packed = jnp.where(lane == 2 * p, slot_max, packed)
        packed = jnp.where(lane == 2 * p + 1, slot_sum, packed)
    pbuf[pages] = jnp.zeros(flat, jnp.bfloat16)
    turned = jnp.concatenate(
        [packed, jnp.zeros((HEAD_DIM - heads, HEAD_DIM), jnp.float32)], axis=0
    ).T
    row = lax.broadcasted_iota(jnp.int32, (8, HEAD_DIM), 0)
    part = lax.rem(row, 4)
    for p in range(pages):
        local = lax.rem(req_ref[p], req_dev).astype(jnp.float32)
        tile = jnp.where(part == 0, turned[2 * p:2 * p + 1], turned[2 * p + 1:2 * p + 2])
        stat[p] = jnp.where(part >= 2, local, tile)
    stat[pages] = jnp.where(part == 0, FLOOR, jnp.where(part == 1, 0.0, -1.0))

    def build(g, _):
        first = leaders[SLOTS * g]
        second = leaders[SLOTS * g + 1]
        sstat[g] = jnp.where(row < 4, stat[first], stat[second])
        sdata[g, 0] = pbuf[first]
        sdata[g, 1] = pbuf[second]
        return 0

    lax.fori_loop(0, n, build, 0)

    def stat_copy(owner, peer):
        return remote(sstat.at[peer], rstat.at[owner], s_send.at[peer], s_recv.at[owner], peer)

    def data_copy(owner, peer):
        return remote(sdata.at[peer], rdata.at[owner], d_send.at[peer], d_recv.at[owner], peer)

    def send_stat(d, _):
        stat_copy(me, lax.rem(me + d, n)).start()
        return 0

    def send_data(d, _):
        data_copy(me, lax.rem(me + d, n)).start()
        return 0

    lax.fori_loop(1, n, send_stat, 0)
    lax.fori_loop(1, n, send_data, 0)
    rstat[me] = sstat[me]
    rdata[me] = sdata[me]

    def wait_stat(d, _):
        owner = lax.rem(me + n - d, n)
        stat_copy(owner, owner).wait_recv()
        return 0

    lax.fori_loop(1, n, wait_stat, 0)

    rows = 8 * n
    got = rstat[...].reshape(rows, HEAD_DIM)
    got_sum = pltpu.roll(got, rows - 1, 0)
    got_id = pltpu.roll(got, rows - 2, 0)
    got_part = lax.rem(lax.broadcasted_iota(jnp.int32, got.shape, 0), 4)
    real = got_part == 0
    ids = jnp.where(real, got_id, -1.0)
    level = jnp.zeros_like(got)
    for r in range(req_dev):
        hit = ids == r
        best = jnp.max(jnp.where(hit, got, FLOOR), axis=0, keepdims=True)
        level = jnp.where(hit, best, level)
    share = jnp.where(ids >= 0.0, got_sum * jnp.exp(jnp.minimum(got - level, 0.0)), 0.0)
    whole = jnp.ones_like(got)
    for r in range(req_dev):
        hit = ids == r
        denom = jnp.sum(jnp.where(hit, share, 0.0), axis=0, keepdims=True)
        whole = jnp.where(hit, denom, whole)
    table = jnp.where(real, share / whole, got).T[:heads]

    def wait_data(d, _):
        owner = lax.rem(me + n - d, n)
        data_copy(owner, owner).wait_recv()
        return 0

    lax.fori_loop(1, n, wait_data, 0)
    totals = [jnp.zeros((heads // 8, 8, HEAD_DIM), jnp.float32) for _ in range(req_dev)]
    for s in range(n):
        for j in range(SLOTS):
            at = 8 * s + 4 * j
            weight = jnp.broadcast_to(table[:, at:at + 1], flat)
            ident = jnp.broadcast_to(table[:8, at + 2:at + 3], (8, HEAD_DIM))
            term = (weight * rdata[s, j].astype(jnp.float32)).reshape(heads // 8, 8, HEAD_DIM)
            for r in range(req_dev):
                totals[r] += jnp.where((ident == r)[None], term, 0.0)
    for r in range(req_dev):
        o_ref[r] = totals[r].reshape(flat).astype(jnp.bfloat16)

    def done_far(k, _):
        far_copy(k, me, sibling).wait_send()
        pair_copy(k, me).wait_send()
        return 0

    lax.fori_loop(1, far_n, done_far, 0)
    pair_copy(0, me).wait_send()

    def done_sib(k, _):
        sib_copy(k, me).wait_send()
        return 0

    lax.fori_loop(0, n // 2, done_sib, 0)

    def done_out(d, _):
        peer = lax.rem(me + d, n)
        stat_copy(me, peer).wait_send()
        data_copy(me, peer).wait_send()
        return 0

    lax.fori_loop(1, n, done_out, 0)


def body(n, queries, keys, values, page_request, page_fill):
    req_dev, width = queries.shape
    pages, page_len, kv_width = keys.shape
    heads = width // HEAD_DIM
    row = (heads, HEAD_DIM)
    dma = pltpu.SemaphoreType.DMA
    smem = pl.BlockSpec(memory_space=pltpu.SMEM)
    vmem = pl.BlockSpec(memory_space=pltpu.VMEM)
    hbm = pl.BlockSpec(memory_space=pl.ANY)
    out = pl.pallas_call(
        functools.partial(kernel, n),
        out_shape=jax.ShapeDtypeStruct((req_dev,) + row, jnp.bfloat16),
        in_specs=[smem, smem, vmem, hbm, hbm],
        out_specs=vmem,
        scratch_shapes=[
            pltpu.VMEM((pages, page_len, kv_width), jnp.bfloat16),
            pltpu.VMEM((pages, page_len, kv_width), jnp.bfloat16),
            pltpu.VMEM((n, req_dev) + row, jnp.bfloat16),
            pltpu.VMEM((pages,) + row, jnp.float32),
            pltpu.VMEM((pages + 1,) + row, jnp.bfloat16),
            pltpu.VMEM((pages + 1, 8, HEAD_DIM), jnp.float32),
            pltpu.VMEM((n, SLOTS) + row, jnp.bfloat16),
            pltpu.VMEM((n, 8, HEAD_DIM), jnp.float32),
            pltpu.VMEM((n, SLOTS) + row, jnp.bfloat16),
            pltpu.VMEM((n, 8, HEAD_DIM), jnp.float32),
            pltpu.SMEM((SLOTS * n,), jnp.int32),
            dma((pages,)), dma((pages,)), dma((n,)), dma((n // 4,)), dma((n // 4,)),
            dma((n // 2,)), dma((n,)), dma((n,)), dma((n,)), dma((n,)),
        ],
        compiler_params=pltpu.CompilerParams(collective_id=0, has_side_effects=True),
    )(page_request, page_fill, queries, keys, values)
    return out.reshape(req_dev, width)


def solution(mesh):
    rows = P(("cell", "seq"))
    return jax.shard_map(
        functools.partial(body, mesh.shape["seq"]), mesh=mesh,
        in_specs=(rows, rows, rows, rows, rows), out_specs=rows, check_vma=False,
    )
```

time: 84 us -> 35.5 us (0.42)
  the two profiles are of different devices: /device:TPU:0 before, /device:TPU:15 now
where the time goes in v1:
time: 35.5 us; the launch traced here: 34.9 us
  Pallas kernels  33.5 us (94%)
  local copies, waits for them, and re-layouts  1.44 us (4%)
    pallas_call x1, Pallas kernels, body(): pl.pallas_call(functools.partial(kernel, n), out_shape=jax.ShapeDtypeStru...  33.5 us
    unnamed x1, local copies, waits for them, and re-layouts  1.44 us

profile of v1, /device:TPU:15, one launch (start us, length us, event | category | flops | bytes accessed | tf_op | source)
XLA Modules:
  0.0 34.9 jit_solution(4264175602642723162)
XLA Ops:
  0.0 33.5 %shard_map.55 = bf16[4,48,128]{2,1,0:T(8,128)(2,1)} custom-call(s32[8]{0:T(128)} %req_ref.1, s32[8]{0:T(128)} %fill_ref.1, bf16[4,6144]{1,0:T(4,128)(2,1)} %q_ref.1, bf16[8,128,1024]{2,1,0:T(8,128)(2,1)} %k_hbm.1, bf16[8,128,1024]{2,1,0:T(8,128)(2,1)} %v_hbm.1), custom_call_target="tpu_custom_call" | custom-call | tf_op jit(solution)/shard_map/pallas_call | solution.py:277
  33.5 1.4 %copy.8 = bf16[1,4,48,128]{3,1,2,0:T(4,128)(2,1)} copy(bf16[1,4,48,128]{3,2,1,0:T(8,128)(2,1)} %bitcast.4) | data formatting | bytes 98304

commit v2 on v1

v2 whole, which is shorter than its diff:
```python
import functools

import jax
import jax.numpy as jnp
from jax import lax
from jax.experimental import pallas as pl
from jax.experimental.pallas import tpu as pltpu
from jax.sharding import PartitionSpec as P

HEAD_DIM = 128
KV_HEADS = 8
FLOOR = -30000.0
SLOTS = 2
PARTS = 2


def kernel(
    n, req_ref, fill_ref, q_ref, k_hbm, v_hbm, o_ref,
    kbuf, vbuf, qbuf0, qbuf1, acc, pbuf, stat, sdata, sstat, rdata, rstat, leaders,
    k_sem, v_sem, q_recv, q_far, q_pair, q_sib, d_send, d_recv, s_send, s_recv,
):
    pages = k_hbm.shape[0]
    req_dev, width = q_ref.shape
    heads = width // HEAD_DIM
    group = heads // KV_HEADS
    part_heads = heads // PARTS
    part_keys = KV_HEADS // PARTS
    span = part_keys * HEAD_DIM
    far_n = n // 4
    me = lax.axis_index("seq")
    qbuf = (qbuf0, qbuf1)

    def remote(src, dst, send, recv, peer):
        return pltpu.make_async_remote_copy(
            src_ref=src, dst_ref=dst, send_sem=send, recv_sem=recv,
            device_id={"seq": peer}, device_id_type=pl.DeviceIdType.MESH,
        )

    barrier = pltpu.get_barrier_semaphore()

    def greet(d, _):
        pl.semaphore_signal(
            barrier, inc=1, device_id={"seq": lax.rem(me + d, n)},
            device_id_type=pl.DeviceIdType.MESH,
        )
        return 0

    lax.fori_loop(1, n, greet, 0)
    for p in range(pages):
        pltpu.make_async_copy(k_hbm.at[p], kbuf.at[p], k_sem.at[p]).start()
    for p in range(pages):
        pltpu.make_async_copy(v_hbm.at[p], vbuf.at[p], v_sem.at[p]).start()

    mine = q_ref[...].astype(jnp.float32)
    mine = mine.reshape(req_dev, heads, HEAD_DIM)
    for h in range(PARTS):
        qbuf[h][me] = mine[:, h * part_heads:(h + 1) * part_heads].astype(jnp.bfloat16)
    pl.semaphore_wait(barrier, n - 1)

    far = me // 4
    place = lax.rem(me, 4)
    other = lax.rem(place + 2, 4)
    pair = far * 4 + other
    sibling = me + 1 - 2 * lax.rem(me, 2)

    def far_copy(h, k, owner, peer):
        block = qbuf[h].at[owner]
        return remote(block, block, q_far.at[h, k], q_recv.at[h, owner], peer)

    def pair_copy(h, k, owner):
        block = qbuf[h].at[owner]
        return remote(block, block, q_pair.at[h, k], q_recv.at[h, owner], pair)

    def sib_copy(h, k, owner):
        block = qbuf[h].at[owner]
        return remote(block, block, q_sib.at[h, k], q_recv.at[h, owner], sibling)

    for h in range(PARTS):
        def start_far(k, _):
            far_copy(h, k, me, lax.rem(far + k, far_n) * 4 + place).start()
            return 0

        lax.fori_loop(1, far_n, start_far, 0)
        pair_copy(h, 0, me).start()
        sib_copy(h, 0, me).start()

    def lead(g, _):
        first = jnp.int32(pages)
        held = jnp.int32(-1)
        for p in reversed(range(pages)):
            hit = req_ref[p] // req_dev == g
            first = jnp.where(hit, p, first)
            held = jnp.where(hit, req_ref[p], held)
        second = jnp.int32(pages)
        for p in reversed(range(pages)):
            hit = jnp.logical_and(req_ref[p] // req_dev == g, req_ref[p] != held)
            second = jnp.where(hit, p, second)
        leaders[SLOTS * g] = first
        leaders[SLOTS * g + 1] = second
        return 0

    lax.fori_loop(0, n, lead, 0)

    def pass_far(h):
        def step(k, _):
            owner = lax.rem(far + far_n - k, far_n) * 4 + place
            far_copy(h, k, owner, owner).wait_recv()
            pair_copy(h, k, owner).start()
            sib_copy(h, k, owner).start()
            return 0

        lax.fori_loop(1, far_n, step, 0)

    def pass_pair(h):
        def step(k, _):
            owner = lax.rem(far + far_n - k, far_n) * 4 + other
            pair_copy(h, k, owner).wait_recv()
            sib_copy(h, far_n + k, owner).start()
            return 0

        lax.fori_loop(0, far_n, step, 0)

    def wait_sib(h):
        def step(k, _):
            sib_copy(h, k, 2 * k + lax.rem(sibling, 2)).wait_recv()
            return 0

        lax.fori_loop(0, n // 2, step, 0)

    flat = (part_heads, HEAD_DIM)
    lane = lax.broadcasted_iota(jnp.int32, flat, 1)
    key_head = lax.broadcasted_iota(jnp.int32, flat, 0) // group

    def attend(h, p):
        r = req_ref[p]
        q = qbuf[h][r // req_dev, lax.rem(r, req_dev)]
        wide = jnp.concatenate(
            [jnp.where(key_head == k, q, jnp.zeros_like(q)) for k in range(part_keys)], axis=1
        )
        if h == 0:
            pltpu.make_async_copy(k_hbm.at[p], kbuf.at[p], k_sem.at[p]).wait()
            pltpu.make_async_copy(v_hbm.at[p], vbuf.at[p], v_sem.at[p]).wait()
        score = lax.dot_general(
            wide, kbuf[p, :, h * span:(h + 1) * span], (((1,), (1,)), ((), ())),
            preferred_element_type=jnp.float32,
        ) * HEAD_DIM ** (-0.5)
        live = lax.broadcasted_iota(jnp.int32, score.shape, 1) < fill_ref[p]
        top = jnp.max(jnp.where(live, score, FLOOR), axis=1, keepdims=True)
        weight = jnp.where(live, jnp.exp(score - top), 0.0).astype(jnp.bfloat16)
        total = jnp.sum(weight.astype(jnp.float32), axis=1, keepdims=True)
        mixed = jnp.dot(
            weight, vbuf[p, :, h * span:(h + 1) * span], preferred_element_type=jnp.float32
        )
        out = jnp.zeros(flat, jnp.float32)
        for k in range(part_keys):
            out = jnp.where(key_head == k, mixed[:, k * HEAD_DIM:(k + 1) * HEAD_DIM], out)
        acc[h, p] = out
        return jnp.broadcast_to(top, flat), jnp.broadcast_to(total, flat)

    row = lax.broadcasted_iota(jnp.int32, (8, HEAD_DIM), 0)
    part = lax.rem(row, 4)

    def merge(h, maxes, sums):
        packed = jnp.zeros(flat, jnp.float32)
        for p in range(pages):
            same = [req_ref[p] == req_ref[q] for q in range(pages)]
            slot_max = jnp.full(flat, FLOOR, jnp.float32)
            for q in range(pages):
                slot_max = jnp.maximum(slot_max, jnp.where(same[q], maxes[q], FLOOR))
            slot_sum = jnp.zeros(flat, jnp.float32)
            slot_acc = jnp.zeros(flat, jnp.float32)
            for q in range(pages):
                factor = jnp.where(same[q], jnp.exp(maxes[q] - slot_max), 0.0)
                slot_sum += factor * sums[q]
                slot_acc += factor * acc[h, q]
            pbuf[h, p] = (slot_acc / jnp.maximum(slot_sum, 1.0)).astype(jnp.bfloat16)
            packed = jnp.where(lane == 2 * p, slot_max, packed)
            packed = jnp.where(lane == 2 * p + 1, slot_sum, packed)
        pbuf[h, pages] = jnp.zeros(flat, jnp.bfloat16)
        turned = jnp.concatenate(
            [packed, jnp.zeros((HEAD_DIM - part_heads, HEAD_DIM), jnp.float32)], axis=0
        ).T
        for p in range(pages):
            local = lax.rem(req_ref[p], req_dev).astype(jnp.float32)
            tile = jnp.where(part == 0, turned[2 * p:2 * p + 1], turned[2 * p + 1:2 * p + 2])
            stat[h, p] = jnp.where(part >= 2, local, tile)
        stat[h, pages] = jnp.where(part == 0, FLOOR, jnp.where(part == 1, 0.0, -1.0))

        def build(g, _):
            first = leaders[SLOTS * g]
            second = leaders[SLOTS * g + 1]
            sstat[h, g] = jnp.where(row < 4, stat[h, first], stat[h, second])
            sdata[h, g, 0] = pbuf[h, first]
            sdata[h, g, 1] = pbuf[h, second]
            return 0

        lax.fori_loop(0, n, build, 0)

    def stat_copy(h, owner, peer):
        return remote(
            sstat.at[h, peer], rstat.at[h, owner], s_send.at[h, peer], s_recv.at[h, owner], peer
        )

    def data_copy(h, owner, peer):
        return remote(
            sdata.at[h, peer], rdata.at[h, owner], d_send.at[h, peer], d_recv.at[h, owner], peer
        )

    def send(h):
        def step(d, _):
            stat_copy(h, me, lax.rem(me + d, n)).start()
            data_copy(h, me, lax.rem(me + d, n)).start()
            return 0

        lax.fori_loop(1, n, step, 0)
        rstat[h, me] = sstat[h, me]
        rdata[h, me] = sdata[h, me]

    def combine(h):
        def wait_stat(d, _):
            owner = lax.rem(me + n - d, n)
            stat_copy(h, owner, owner).wait_recv()
            return 0

        lax.fori_loop(1, n, wait_stat, 0)
        rows = 8 * n
        got = rstat[h].reshape(rows, HEAD_DIM)
        got_sum = pltpu.roll(got, rows - 1, 0)
        got_id = pltpu.roll(got, rows - 2, 0)
        got_part = lax.rem(lax.broadcasted_iota(jnp.int32, got.shape, 0), 4)
        real = got_part == 0
        ids = jnp.where(real, got_id, -1.0)
        level = jnp.zeros_like(got)
        for r in range(req_dev):
            hit = ids == r
            best = jnp.max(jnp.where(hit, got, FLOOR), axis=0, keepdims=True)
            level = jnp.where(hit, best, level)
        share = jnp.where(ids >= 0.0, got_sum * jnp.exp(jnp.minimum(got - level, 0.0)), 0.0)
        whole = jnp.ones_like(got)
        for r in range(req_dev):
            hit = ids == r
            denom = jnp.sum(jnp.where(hit, share, 0.0), axis=0, keepdims=True)
            whole = jnp.where(hit, denom, whole)
        table = jnp.where(real, share / whole, got).T[:part_heads]

        def wait_data(d, _):
            owner = lax.rem(me + n - d, n)
            data_copy(h, owner, owner).wait_recv()
            return 0

        lax.fori_loop(1, n, wait_data, 0)
        totals = [jnp.zeros((part_heads // 8, 8, HEAD_DIM), jnp.float32) for _ in range(req_dev)]
        for s in range(n):
            for j in range(SLOTS):
                at = 8 * s + 4 * j
                weight = jnp.broadcast_to(table[:, at:at + 1], flat)
                ident = jnp.broadcast_to(table[:8, at + 2:at + 3], (8, HEAD_DIM))
                term = (weight * rdata[h, s, j].astype(jnp.float32)).reshape(part_heads // 8, 8, HEAD_DIM)
                for r in range(req_dev):
                    totals[r] += jnp.where((ident == r)[None], term, 0.0)
        return [total.reshape(flat) for total in totals]

    pass_far(0)
    pass_pair(0)
    pass_far(1)
    wait_sib(0)
    found = [attend(0, p) for p in range(pages // 2)]
    pass_pair(1)
    found += [attend(0, p) for p in range(pages // 2, pages)]
    merge(0, [f[0] for f in found], [f[1] for f in found])
    send(0)
    wait_sib(1)
    found = [attend(1, p) for p in range(pages)]
    merge(1, [f[0] for f in found], [f[1] for f in found])
    send(1)
    merged = [combine(h) for h in range(PARTS)]
    for r in range(req_dev):
        o_ref[r] = jnp.concatenate([m[r] for m in merged], axis=0).astype(jnp.bfloat16)

    for h in range(PARTS):
        def done_far(k, _):
            far_copy(h, k, me, sibling).wait_send()
            pair_copy(h, k, me).wait_send()
            return 0

        def done_sib(k, _):
            sib_copy(h, k, me).wait_send()
            return 0

        def done_out(d, _):
            peer = lax.rem(me + d, n)
            stat_copy(h, me, peer).wait_send()
            data_copy(h, me, peer).wait_send()
            return 0

        lax.fori_loop(1, far_n, done_far, 0)
        pair_copy(h, 0, me).wait_send()
        lax.fori_loop(0, n // 2, done_sib, 0)
        lax.fori_loop(1, n, done_out, 0)


def body(n, queries, keys, values, page_request, page_fill):
    req_dev, width = queries.shape
    pages, page_len, kv_width = keys.shape
    heads = width // HEAD_DIM
    row = (heads, HEAD_DIM)
    part = (heads // PARTS, HEAD_DIM)
    dma = pltpu.SemaphoreType.DMA
    smem = pl.BlockSpec(memory_space=pltpu.SMEM)
    vmem = pl.BlockSpec(memory_space=pltpu.VMEM)
    hbm = pl.BlockSpec(memory_space=pl.ANY)
    out = pl.pallas_call(
        functools.partial(kernel, n),
        out_shape=jax.ShapeDtypeStruct((req_dev,) + row, jnp.bfloat16),
        in_specs=[smem, smem, vmem, hbm, hbm],
        out_specs=vmem,
        scratch_shapes=[
            pltpu.VMEM((pages, page_len, kv_width), jnp.bfloat16),
            pltpu.VMEM((pages, page_len, kv_width), jnp.bfloat16),
            pltpu.VMEM((n, req_dev) + part, jnp.bfloat16),
            pltpu.VMEM((n, req_dev) + part, jnp.bfloat16),
            pltpu.VMEM((PARTS, pages) + part, jnp.float32),
            pltpu.VMEM((PARTS, pages + 1) + part, jnp.bfloat16),
            pltpu.VMEM((PARTS, pages + 1, 8, HEAD_DIM), jnp.float32),
            pltpu.VMEM((PARTS, n, SLOTS) + part, jnp.bfloat16),
            pltpu.VMEM((PARTS, n, 8, HEAD_DIM), jnp.float32),
            pltpu.VMEM((PARTS, n, SLOTS) + part, jnp.bfloat16),
            pltpu.VMEM((PARTS, n, 8, HEAD_DIM), jnp.float32),
            pltpu.SMEM((SLOTS * n,), jnp.int32),
            dma((pages,)), dma((pages,)), dma((PARTS, n)), dma((PARTS, n // 4)),
            dma((PARTS, n // 4)), dma((PARTS, n // 2)), dma((PARTS, n)), dma((PARTS, n)),
            dma((PARTS, n)), dma((PARTS, n)),
        ],
        compiler_params=pltpu.CompilerParams(collective_id=0, has_side_effects=True),
    )(page_request, page_fill, queries, keys, values)
    return out.reshape(req_dev, width)


def solution(mesh):
    rows = P(("cell", "seq"))
    return jax.shard_map(
        functools.partial(body, mesh.shape["seq"]), mesh=mesh,
        in_specs=(rows, rows, rows, rows, rows), out_specs=rows, check_vma=False,
    )
```

time: 35.5 us -> 36.3 us (1.023)
  the two profiles are of different devices: /device:TPU:15 before, /device:TPU:0 now
where the time goes in v2:
time: 36.3 us; the launch traced here: 36.1 us
  Pallas kernels  34.7 us (96%)
  local copies, waits for them, and re-layouts  1.44 us (4%)
    pallas_call x1, Pallas kernels, body(): pl.pallas_call(functools.partial(kernel, n), out_shape=jax.ShapeDtypeStru...  34.7 us
    unnamed x1, local copies, waits for them, and re-layouts  1.44 us

profile of v2, /device:TPU:0, one launch (start us, length us, event | category | flops | bytes accessed | tf_op | source)
XLA Modules:
  0.0 36.1 jit_solution(11113601425545175132)
XLA Ops:
  0.0 34.7 %shard_map.55 = bf16[4,48,128]{2,1,0:T(8,128)(2,1)} custom-call(s32[8]{0:T(128)} %req_ref.1, s32[8]{0:T(128)} %fill_ref.1, bf16[4,6144]{1,0:T(4,128)(2,1)} %q_ref.1, bf16[8,128,1024]{2,1,0:T(8,128)(2,1)} %k_hbm.1, bf16[8,128,1024]{2,1,0:T(8,128)(2,1)} %v_hbm.1), custom_call_target="tpu_custom_call" | custom-call | tf_op jit(solution)/shard_map/pallas_call | solution.py:312
  34.7 1.4 %copy.8 = bf16[1,4,48,128]{3,1,2,0:T(4,128)(2,1)} copy(bf16[1,4,48,128]{3,2,1,0:T(8,128)(2,1)} %bitcast.4) | data formatting | bytes 98304

commit v3 on v1

--- a/solution.py
+++ b/solution.py
@@ -33,28 +33,32 @@
 
     barrier = pltpu.get_barrier_semaphore()
 
-    def greet(d, _):
-        pl.semaphore_signal(
-            barrier, inc=1, device_id={"seq": lax.rem(me + d, n)},
-            device_id_type=pl.DeviceIdType.MESH,
-        )
-        return 0
-
-    lax.fori_loop(1, n, greet, 0)
-    for p in range(pages):
-        pltpu.make_async_copy(k_hbm.at[p], kbuf.at[p], k_sem.at[p]).start()
-    for p in range(pages):
-        pltpu.make_async_copy(v_hbm.at[p], vbuf.at[p], v_sem.at[p]).start()
-
-    mine = q_ref[...].astype(jnp.float32)
-    qbuf[me] = mine.reshape(req_dev, heads, HEAD_DIM).astype(jnp.bfloat16)
-    pl.semaphore_wait(barrier, n - 1)
-
     far = me // 4
     place = lax.rem(me, 4)
     other = lax.rem(place + 2, 4)
     pair = far * 4 + other
     sibling = me + 1 - 2 * lax.rem(me, 2)
+
+    def greet(peer):
+        pl.semaphore_signal(
+            barrier, inc=1, device_id={"seq": peer}, device_id_type=pl.DeviceIdType.MESH
+        )
+
+    def greet_far(k, _):
+        greet(lax.rem(far + k, far_n) * 4 + place)
+        return 0
+
+    lax.fori_loop(1, far_n, greet_far, 0)
+    greet(pair)
+    greet(sibling)
+    for p in range(pages):
+        pltpu.make_async_copy(k_hbm.at[p], kbuf.at[p], k_sem.at[p]).start()
+    for p in range(pages):
+        pltpu.make_async_copy(v_hbm.at[p], vbuf.at[p], v_sem.at[p]).start()
+
+    mine = q_ref[...].astype(jnp.float32)
+    qbuf[me] = mine.reshape(req_dev, heads, HEAD_DIM).astype(jnp.bfloat16)
+    pl.semaphore_wait(barrier, far_n + 1)
 
     def far_copy(k, owner, peer):
         return remote(qbuf.at[owner], qbuf.at[owner], q_far.at[k], q_recv.at[owner], peer)
@@ -114,6 +118,9 @@
 
     lax.fori_loop(0, n // 2, wait_sib, 0)
 
+    for p in range(pages):
+        pltpu.make_async_copy(k_hbm.at[p], kbuf.at[p], k_sem.at[p]).wait()
+        pltpu.make_async_copy(v_hbm.at[p], vbuf.at[p], v_sem.at[p]).wait()
     lane = lax.broadcasted_iota(jnp.int32, (heads, HEAD_DIM), 1)
     key_head = lax.broadcasted_iota(jnp.int32, (heads, HEAD_DIM), 0) // group
     flat = (heads, HEAD_DIM)
@@ -124,7 +131,6 @@
         wide = jnp.concatenate(
             [jnp.where(key_head == k, q, jnp.zeros_like(q)) for k in range(KV_HEADS)], axis=1
         )
-        pltpu.make_async_copy(k_hbm.at[p], kbuf.at[p], k_sem.at[p]).wait()
         score = lax.dot_general(
             wide, kbuf[p], (((1,), (1,)), ((), ())), preferred_element_type=jnp.float32
         ) * HEAD_DIM ** (-0.5)
@@ -132,7 +138,6 @@
         top = jnp.max(jnp.where(live, score, FLOOR), axis=1, keepdims=True)
         weight = jnp.where(live, jnp.exp(score - top), 0.0).astype(jnp.bfloat16)
         total = jnp.sum(weight.astype(jnp.float32), axis=1, keepdims=True)
-        pltpu.make_async_copy(v_hbm.at[p], vbuf.at[p], v_sem.at[p]).wait()
         mixed = jnp.dot(weight, vbuf[p], preferred_element_type=jnp.float32)
         out = jnp.zeros(flat, jnp.float32)
         for k in range(KV_HEADS):

time: 35.5 us -> 32.7 us (0.921)
  Pallas kernels: 33.5 us -> 31 us
    pallas_call x1, Pallas kernels: 33.5 us -> 31 us  [body(): pl.pallas_call(functools.partial(kernel, n), out_shape=jax.ShapeDtypeStru...]
where the time goes in v3:
time: 32.7 us; the launch traced here: 32.4 us
  Pallas kernels  31 us (95%)
  local copies, waits for them, and re-layouts  1.44 us (4%)
    pallas_call x1, Pallas kernels, body(): pl.pallas_call(functools.partial(kernel, n), out_shape=jax.ShapeDtypeStru...  31 us
    unnamed x1, local copies, waits for them, and re-layouts  1.44 us

profile of v3, /device:TPU:15, one launch (start us, length us, event | category | flops | bytes accessed | tf_op | source)
XLA Modules:
  0.0 32.4 jit_solution(5975239056186555630)
XLA Ops:
  0.0 31.0 %shard_map.55 = bf16[4,48,128]{2,1,0:T(8,128)(2,1)} custom-call(s32[8]{0:T(128)} %req_ref.1, s32[8]{0:T(128)} %fill_ref.1, bf16[4,6144]{1,0:T(4,128)(2,1)} %q_ref.1, bf16[8,128,1024]{2,1,0:T(8,128)(2,1)} %k_hbm.1, bf16[8,128,1024]{2,1,0:T(8,128)(2,1)} %v_hbm.1), custom_call_target="tpu_custom_call" | custom-call | tf_op jit(solution)/shard_map/pallas_call | solution.py:282
  31.0 1.4 %copy.8 = bf16[1,4,48,128]{3,1,2,0:T(4,128)(2,1)} copy(bf16[1,4,48,128]{3,2,1,0:T(8,128)(2,1)} %bitcast.4) | data formatting | bytes 98304

commit v4 on v3

--- a/solution.py
+++ b/solution.py
@@ -244,8 +244,8 @@
             term = (weight * rdata[s, j].astype(jnp.float32)).reshape(heads // 8, 8, HEAD_DIM)
             for r in range(req_dev):
                 totals[r] += jnp.where((ident == r)[None], term, 0.0)
-    for r in range(req_dev):
-        o_ref[r] = totals[r].reshape(flat).astype(jnp.bfloat16)
+    rows_out = jnp.concatenate([t.reshape((1,) + flat) for t in totals], axis=0)
+    o_ref[...] = rows_out.reshape(req_dev, width).astype(jnp.bfloat16)
 
     def done_far(k, _):
         far_copy(k, me, sibling).wait_send()
@@ -281,7 +281,7 @@
     hbm = pl.BlockSpec(memory_space=pl.ANY)
     out = pl.pallas_call(
         functools.partial(kernel, n),
-        out_shape=jax.ShapeDtypeStruct((req_dev,) + row, jnp.bfloat16),
+        out_shape=jax.ShapeDtypeStruct((req_dev, width), jnp.bfloat16),
         in_specs=[smem, smem, vmem, hbm, hbm],
         out_specs=vmem,
         scratch_shapes=[
@@ -301,7 +301,7 @@
         ],
         compiler_params=pltpu.CompilerParams(collective_id=0, has_side_effects=True),
     )(page_request, page_fill, queries, keys, values)
-    return out.reshape(req_dev, width)
+    return out
 
 
 def solution(mesh):

time: 32.7 us -> 32.7 us (level)
  no operation moved by 1% of the time
where the time goes in v4:
time: 32.7 us; the launch traced here: 32.5 us
  Pallas kernels  31 us (95%)
  local copies, waits for them, and re-layouts  1.44 us (4%)
    pallas_call x1, Pallas kernels, body(): pl.pallas_call(functools.partial(kernel, n), out_shape=jax.ShapeDtypeStru...  31 us
    unnamed x1, local copies, waits for them, and re-layouts  1.44 us

profile of v4, /device:TPU:15, one launch (start us, length us, event | category | flops | bytes accessed | tf_op | source)
XLA Modules:
  0.0 32.5 jit_solution(8276605149163144853)
XLA Ops:
  0.0 31.0 %shard_map.55 = bf16[4,6144]{1,0:T(4,128)(2,1)} custom-call(s32[8]{0:T(128)} %req_ref.1, s32[8]{0:T(128)} %fill_ref.1, bf16[4,6144]{1,0:T(4,128)(2,1)} %q_ref.1, bf16[8,128,1024]{2,1,0:T(8,128)(2,1)} %k_hbm.1, bf16[8,128,1024]{2,1,0:T(8,128)(2,1)} %v_hbm.1), custom_call_target="tpu_custom_call" | custom-call | tf_op jit(solution)/shard_map/pallas_call | solution.py:282
  31.0 1.4 %copy.7 = bf16[4,6144]{1,0:T(4,128)(2,1)} copy(bf16[4,6144]{1,0:T(4,128)(2,1)} %shard_map.55) | data formatting | bytes 98304

commit v5 on v3

--- a/solution.py
+++ b/solution.py
@@ -181,7 +181,7 @@
         sdata[g, 1] = pbuf[second]
         return 0
 
-    lax.fori_loop(0, n, build, 0)
+    lax.fori_loop(0, n, build, 0, unroll=4)
 
     def stat_copy(owner, peer):
         return remote(sstat.at[peer], rstat.at[owner], s_send.at[peer], s_recv.at[owner], peer)

time: 32.7 us -> 32.6 us (level)
  no operation moved by 1% of the time
where the time goes in v5:
time: 32.6 us; the launch traced here: 32.4 us
  Pallas kernels  30.9 us (95%)
  local copies, waits for them, and re-layouts  1.44 us (4%)
    pallas_call x1, Pallas kernels, body(): pl.pallas_call(functools.partial(kernel, n), out_shape=jax.ShapeDtypeStru...  30.9 us
    unnamed x1, local copies, waits for them, and re-layouts  1.44 us

profile of v5, /device:TPU:15, one launch (start us, length us, event | category | flops | bytes accessed | tf_op | source)
XLA Modules:
  0.0 32.4 jit_solution(9796560371963815983)
XLA Ops:
  0.0 30.9 %shard_map.55 = bf16[4,48,128]{2,1,0:T(8,128)(2,1)} custom-call(s32[8]{0:T(128)} %req_ref.1, s32[8]{0:T(128)} %fill_ref.1, bf16[4,6144]{1,0:T(4,128)(2,1)} %q_ref.1, bf16[8,128,1024]{2,1,0:T(8,128)(2,1)} %k_hbm.1, bf16[8,128,1024]{2,1,0:T(8,128)(2,1)} %v_hbm.1), custom_call_target="tpu_custom_call" | custom-call | tf_op jit(solution)/shard_map/pallas_call | solution.py:282
  30.9 1.4 %copy.8 = bf16[1,4,48,128]{3,1,2,0:T(4,128)(2,1)} copy(bf16[1,4,48,128]{3,2,1,0:T(8,128)(2,1)} %bitcast.4) | data formatting | bytes 98304
